TPU v7x, 32 devices: a whole 2x2x4 slice. The times are simulated.
32 devices in a mesh: samp: 8 (over z, y), feat: 4 (over x, core).
Axes of the slice: x: 2, y: 2, z: 4, core: 2. Of those that a mesh axis runs over, the one named last changes fastest.
Arguments:
- layer_input: bfloat16 [512, 64, 512], P('samp', 'feat'), may hold values from -6 to 6
- segment_ids: int32 [512], replicated, may hold values from 0 to 3, as said below
- context_flags: int32 [512], replicated, may hold values from 0 to 1, as said below
- first_gain: float32 [512], replicated, may hold values from 0.1 to 1.9
- first_shift: float32 [512], replicated, may hold values from -3 to 3
- sample_weight: bfloat16 [512, 1536], replicated, may hold values from -0.25 to 0.25
- sample_bias: float32 [1024], replicated, may hold values from -3 to 3
- sample_mixer: bfloat16 [512, 512], replicated, may hold values from -1 to 1
- sample_offset: float32 [512], replicated, may hold values from -3 to 3
- second_gain: float32 [512], replicated, may hold values from 0.1 to 1.9
- second_shift: float32 [512], replicated, may hold values from -3 to 3
- feature_weight: bfloat16 [512, 1536], replicated, may hold values from -0.25 to 0.25
- feature_bias: float32 [1024], replicated, may hold values from -3 to 3
- feature_mixer: bfloat16 [512, 512], replicated, may hold values from -1.5 to 1.5
- feature_offset: float32 [512], replicated, may hold values from -3 to 3
- third_gain: float32 [512], replicated, may hold values from 0.1 to 1.9
- third_shift: float32 [512], replicated, may hold values from -3 to 3
- expand_weight: bfloat16 [512, 2048], replicated, may hold values from -0.25 to 0.25
- expand_bias: float32 [2048], replicated, may hold values from -3 to 3
- reduce_weight: bfloat16 [2048, 512], replicated, may hold values from -0.125 to 0.125
- reduce_bias: float32 [512], replicated, may hold values from -3 to 3
- cotangent: bfloat16 [512, 64, 512], P('samp', 'feat'), may hold values from -6 to 6
Outputs:
- layer_output: bfloat16 [512, 64, 512], P('samp', 'feat')
- input_grad: bfloat16 [512, 64, 512], P('samp', 'feat')
- first_gain_grad: float32 [512], P('samp')
- first_shift_grad: float32 [512], P('samp')
- sample_weight_grad: float32 [512, 1536], P('samp')
- sample_bias_grad: float32 [1024], P('samp')
- sample_mixer_grad: float32 [512, 512], P('samp')
- sample_offset_grad: float32 [512], P('samp')
- second_gain_grad: float32 [512], P('samp')
- second_shift_grad: float32 [512], P('samp')
- feature_weight_grad: float32 [512, 1536], P('samp')
- feature_bias_grad: float32 [1024], P('samp')
- feature_mixer_grad: float32 [512, 512], P('samp')
- feature_offset_grad: float32 [512], P('samp')
- third_gain_grad: float32 [512], P('samp')
- third_shift_grad: float32 [512], P('samp')
- expand_weight_grad: float32 [512, 2048], P('samp')
- expand_bias_grad: float32 [2048], P('samp')
- reduce_weight_grad: float32 [2048, 512], P('samp')
- reduce_bias_grad: float32 [512], P('samp')
Inputs may be any that keep to these rules, and one draw needn't show every extreme that they name: `context_flags`: the samples of one index of samp (an aligned block of 64 samples) are all context samples or all query samples; exactly 1 block are context blocks, which ones is drawn. `segment_ids`: every task holds exactly 16 context samples.
All inputs are finite; a program needn't handle non-finite values.
Results may differ from a plain program's by a relative error of at most 0.017.
Values may be sent and summed in bfloat16 or wider, within the bound.
No kernel may reach another device: no remote copies, remote signals or barrier semaphores. Data moves between devices by JAX's collectives and lax.ppermute only.
A program may use at most 256 MiB of HBM per device.

v0:
```python
from functools import partial
import jax
import jax.numpy as jnp
from jax import lax
from jax.sharding import PartitionSpec as P

HEADS = 8
HEAD_DIM = 64
EPS = 1e-05
MASKED = -1000000000.0


def spread_2(block, axis, owner):
    block = jnp.where(lax.axis_index(axis) == owner, block, jnp.zeros_like(block))
    return lax.psum(block, axis)


def layer_norm(values, gain_row, shift_row):
    center = jnp.mean(values, axis=-1, keepdims=True)
    spread = values - center
    variance = jnp.mean(spread * spread, axis=-1, keepdims=True)
    return spread * lax.rsqrt(variance + EPS) * gain_row + shift_row


def apply_weight(active, weight):
    return jnp.einsum("sfd,de->sfe", active, weight, preferred_element_type=jnp.float32)


def input_back(grad_out, weight):
    return jnp.einsum("sfe,de->sfd", grad_out, weight, preferred_element_type=jnp.float32)


def weight_grad(active, grad_out):
    return jnp.einsum("sfd,sfe->de", active, grad_out, preferred_element_type=jnp.float32)


def column_sum(values):
    return jnp.sum(values.astype(jnp.float32), axis=(0, 1))


def project(active, weight, bias_row):
    model_width = active.shape[-1]
    joined = apply_weight(active, weight)
    queries = (joined[..., :model_width] + bias_row[:model_width]).astype(jnp.bfloat16)
    key_part = joined[..., model_width : 2 * model_width].astype(jnp.bfloat16)
    value_part = (joined[..., 2 * model_width :] + bias_row[model_width:]).astype(jnp.bfloat16)
    return (queries, key_part, value_part)


def split_heads(values):
    return values.reshape(values.shape[0], values.shape[1], HEADS, HEAD_DIM)


def join_heads(values):
    return values.reshape(values.shape[0], values.shape[1], HEADS * HEAD_DIM)


def soft_weights(scores):
    top_score = jnp.max(scores, axis=-1, keepdims=True)
    raised = jnp.exp(scores - top_score)
    return raised / jnp.sum(raised, axis=-1, keepdims=True)


def feature_attend(queries, key_part, value_part):
    score_scale = HEAD_DIM ** (-0.5)
    scores = (
        jnp.einsum(
            "sfhd,sghd->shfg",
            split_heads(queries),
            split_heads(key_part),
            preferred_element_type=jnp.float32,
        )
        * score_scale
    )
    probability = soft_weights(scores)
    mixed = jnp.einsum(
        "shfg,sghd->sfhd",
        probability.astype(jnp.bfloat16),
        split_heads(value_part),
        preferred_element_type=jnp.float32,
    )
    return (join_heads(mixed).astype(jnp.bfloat16), probability)


def feature_grads(queries, key_part, value_part, probability, grad_mixed):
    score_scale = HEAD_DIM ** (-0.5)
    grad_heads = split_heads(grad_mixed)
    grad_weights = jnp.einsum(
        "sfhd,sghd->shfg", grad_heads, split_heads(value_part), preferred_element_type=jnp.float32
    )
    inner_sum = jnp.sum(probability * grad_weights, axis=-1, keepdims=True)
    grad_scores = (probability * (grad_weights - inner_sum)).astype(jnp.bfloat16)
    grad_queries = (
        jnp.einsum(
            "shfg,sghd->sfhd",
            grad_scores,
            split_heads(key_part),
            preferred_element_type=jnp.float32,
        )
        * score_scale
    )
    grad_keys = (
        jnp.einsum(
            "shfg,sfhd->sghd", grad_scores, split_heads(queries), preferred_element_type=jnp.float32
        )
        * score_scale
    )
    grad_values = jnp.einsum(
        "shfg,sfhd->sghd",
        probability.astype(jnp.bfloat16),
        grad_heads,
        preferred_element_type=jnp.float32,
    )
    return (join_heads(grad_queries), join_heads(grad_keys), join_heads(grad_values))


def local(
    layer_input,
    segment_ids,
    context_flags,
    first_gain,
    first_shift,
    sample_weight,
    sample_bias,
    sample_mixer,
    sample_offset,
    second_gain,
    second_shift,
    feature_weight,
    feature_bias,
    feature_mixer,
    feature_offset,
    third_gain,
    third_shift,
    expand_weight,
    expand_bias,
    reduce_weight,
    reduce_bias,
    cotangent,
):
    sample_rows = layer_input.shape[0]
    feature_rows = layer_input.shape[1]
    model_width = layer_input.shape[2]
    score_scale = HEAD_DIM ** (-0.5)
    shard_count = lax.axis_size("samp")
    context_shards = shard_count // 8
    total_context = context_shards * sample_rows
    residual_zero = layer_input.astype(jnp.float32)
    normed_one, norm_one_back = jax.vjp(layer_norm, residual_zero, first_gain, first_shift)
    active_one = normed_one.astype(jnp.bfloat16)
    queries_one, keys_one, values_one = project(active_one, sample_weight, sample_bias)
    my_index = lax.axis_index("samp")
    shard_flags = context_flags.reshape(shard_count, sample_rows)[:, 0]
    shard_rank = jnp.cumsum(shard_flags) - 1
    shard_ids = jnp.arange(shard_count, dtype=jnp.int32)
    slot_ids = jnp.arange(context_shards, dtype=jnp.int32)
    root_hits = (shard_rank[None, :] == slot_ids[:, None]) & (shard_flags[None, :] == 1)
    roots = jnp.sum(jnp.where(root_hits, shard_ids[None, :], 0), axis=1)
    context_tasks = jnp.take(segment_ids.reshape(shard_count, sample_rows), roots, axis=0).reshape(
        total_context
    )
    local_tasks = lax.dynamic_slice_in_dim(segment_ids, my_index * sample_rows, sample_rows)
    allowed = local_tasks[:, None] == context_tasks[None, :]
    is_context = shard_flags[my_index] == 1
    own_rank = jnp.maximum(shard_rank[my_index], 0)
    own_block = jnp.concatenate([keys_one, values_one], axis=-1)

    def fetch_rows(step, buffer):
        piece = spread_2(own_block, "samp", roots[step])
        return lax.dynamic_update_slice_in_dim(buffer, piece, step * sample_rows, 0)

    empty_rows = jnp.zeros((total_context, feature_rows, 2 * model_width), jnp.bfloat16)
    fetched = lax.fori_loop(0, context_shards, fetch_rows, empty_rows)
    context_keys = fetched[..., :model_width]
    context_values = fetched[..., model_width:]
    query_heads = split_heads(queries_one)
    key_heads = split_heads(context_keys)
    value_heads = split_heads(context_values)
    scores = (
        jnp.einsum("sfhd,cfhd->fhsc", query_heads, key_heads, preferred_element_type=jnp.float32)
        * score_scale
    )
    sample_prob = soft_weights(jnp.where(allowed[None, None], scores, MASKED))
    sample_weights = sample_prob.astype(jnp.bfloat16)
    mixed_one = join_heads(
        jnp.einsum(
            "fhsc,cfhd->sfhd", sample_weights, value_heads, preferred_element_type=jnp.float32
        )
    ).astype(jnp.bfloat16)
    residual_one = residual_zero + apply_weight(mixed_one, sample_mixer) + sample_offset
    normed_two, norm_two_back = jax.vjp(layer_norm, residual_one, second_gain, second_shift)
    active_two = normed_two.astype(jnp.bfloat16)
    queries_two, keys_two, values_two = project(active_two, feature_weight, feature_bias)
    all_keys, all_values = (
        lax.all_gather(keys_two, "feat", axis=1, tiled=True),
        lax.all_gather(values_two, "feat", axis=1, tiled=True),
    )
    mixed_two, feature_prob = feature_attend(queries_two, all_keys, all_values)
    residual_two = residual_one + apply_weight(mixed_two, feature_mixer) + feature_offset
    normed_three, norm_three_back = jax.vjp(layer_norm, residual_two, third_gain, third_shift)
    active_three = normed_three.astype(jnp.bfloat16)
    expanded = apply_weight(active_three, expand_weight) + expand_bias
    activated, gelu_back = jax.vjp(partial(jax.nn.gelu, approximate=False), expanded)
    hidden = activated.astype(jnp.bfloat16)
    layer_output = (residual_two + apply_weight(hidden, reduce_weight) + reduce_bias).astype(
        jnp.bfloat16
    )
    grad_out = cotangent.astype(jnp.float32)
    grad_branch = cotangent
    reduce_bias_grad = column_sum(grad_branch)
    reduce_weight_grad = weight_grad(hidden, grad_branch)
    grad_hidden = input_back(grad_branch, reduce_weight).astype(jnp.bfloat16)
    grad_expanded = gelu_back(grad_hidden.astype(jnp.float32))[0].astype(jnp.bfloat16)
    expand_bias_grad = column_sum(grad_expanded)
    expand_weight_grad = weight_grad(active_three, grad_expanded)
    grad_norm, third_gain_grad, third_shift_grad = norm_three_back(
        input_back(grad_expanded, expand_weight)
    )
    grad_two = grad_out + grad_norm
    grad_branch = grad_two.astype(jnp.bfloat16)
    feature_offset_grad = column_sum(grad_branch)
    feature_mixer_grad = weight_grad(mixed_two, grad_branch)
    grad_mixed = input_back(grad_branch, feature_mixer).astype(jnp.bfloat16)
    grad_queries, grad_keys, grad_values = feature_grads(
        queries_two, all_keys, all_values, feature_prob, grad_mixed
    )
    own_key_grads, own_value_grads = (
        lax.psum_scatter(grad_keys, "feat", scatter_dimension=1, tiled=True),
        lax.psum_scatter(grad_values, "feat", scatter_dimension=1, tiled=True),
    )
    grad_project = jnp.concatenate(
        [
            grad_queries.astype(jnp.bfloat16),
            own_key_grads.astype(jnp.bfloat16),
            own_value_grads.astype(jnp.bfloat16),
        ],
        axis=-1,
    )
    feature_weight_grad = weight_grad(active_two, grad_project)
    feature_bias_grad = jnp.concatenate(
        [
            column_sum(grad_project[..., :model_width]),
            column_sum(grad_project[..., 2 * model_width :]),
        ]
    )
    grad_norm, second_gain_grad, second_shift_grad = norm_two_back(
        input_back(grad_project, feature_weight)
    )
    grad_one = grad_two + grad_norm
    grad_branch = grad_one.astype(jnp.bfloat16)
    sample_offset_grad = column_sum(grad_branch)
    sample_mixer_grad = weight_grad(mixed_one, grad_branch)
    grad_heads = split_heads(input_back(grad_branch, sample_mixer).astype(jnp.bfloat16))
    grad_weights = jnp.einsum(
        "sfhd,cfhd->fhsc", grad_heads, value_heads, preferred_element_type=jnp.float32
    )
    inner_sum = jnp.sum(sample_prob * grad_weights, axis=-1, keepdims=True)
    grad_scores = (sample_prob * (grad_weights - inner_sum)).astype(jnp.bfloat16)
    grad_queries = (
        join_heads(
            jnp.einsum(
                "fhsc,cfhd->sfhd", grad_scores, key_heads, preferred_element_type=jnp.float32
            )
        )
        * score_scale
    ).astype(jnp.bfloat16)
    key_terms = (
        join_heads(
            jnp.einsum(
                "fhsc,sfhd->cfhd", grad_scores, query_heads, preferred_element_type=jnp.float32
            )
        )
        * score_scale
    )
    value_terms = join_heads(
        jnp.einsum(
            "fhsc,sfhd->cfhd", sample_weights, grad_heads, preferred_element_type=jnp.float32
        )
    )
    term_block = jnp.concatenate([key_terms, value_terms], axis=-1)
    summed_terms = lax.psum_scatter(term_block, "samp", scatter_dimension=0, tiled=True)
    summed_rows = lax.all_gather(summed_terms.astype(jnp.bfloat16), "samp", axis=0, tiled=True)
    own_grads = lax.dynamic_slice_in_dim(summed_rows, own_rank * sample_rows, sample_rows, 0)
    own_grads = jnp.where(is_context, own_grads, jnp.zeros_like(own_grads))
    grad_project = jnp.concatenate([grad_queries, own_grads], axis=-1)
    sample_weight_grad = weight_grad(active_one, grad_project)
    sample_bias_grad = jnp.concatenate(
        [column_sum(grad_queries), column_sum(own_grads[..., model_width:])]
    )
    grad_norm, first_gain_grad, first_shift_grad = norm_one_back(
        input_back(grad_project, sample_weight)
    )
    input_grad = (grad_one + grad_norm).astype(jnp.bfloat16)
    summed = lax.psum(
        (
            first_gain_grad,
            first_shift_grad,
            sample_weight_grad,
            sample_bias_grad,
            sample_mixer_grad,
            sample_offset_grad,
            second_gain_grad,
            second_shift_grad,
            feature_weight_grad,
            feature_bias_grad,
            feature_mixer_grad,
            feature_offset_grad,
            third_gain_grad,
            third_shift_grad,
            expand_weight_grad,
            expand_bias_grad,
            reduce_weight_grad,
            reduce_bias_grad,
        ),
        "feat",
    )
    shares = (
        lax.psum_scatter(summed[0], "samp", scatter_dimension=0, tiled=True),
        lax.psum_scatter(summed[1], "samp", scatter_dimension=0, tiled=True),
        lax.psum_scatter(summed[2], "samp", scatter_dimension=0, tiled=True),
        lax.psum_scatter(summed[3], "samp", scatter_dimension=0, tiled=True),
        lax.psum_scatter(summed[4], "samp", scatter_dimension=0, tiled=True),
        lax.psum_scatter(summed[5], "samp", scatter_dimension=0, tiled=True),
        lax.psum_scatter(summed[6], "samp", scatter_dimension=0, tiled=True),
        lax.psum_scatter(summed[7], "samp", scatter_dimension=0, tiled=True),
        lax.psum_scatter(summed[8], "samp", scatter_dimension=0, tiled=True),
        lax.psum_scatter(summed[9], "samp", scatter_dimension=0, tiled=True),
        lax.psum_scatter(summed[10], "samp", scatter_dimension=0, tiled=True),
        lax.psum_scatter(summed[11], "samp", scatter_dimension=0, tiled=True),
        lax.psum_scatter(summed[12], "samp", scatter_dimension=0, tiled=True),
        lax.psum_scatter(summed[13], "samp", scatter_dimension=0, tiled=True),
        lax.psum_scatter(summed[14], "samp", scatter_dimension=0, tiled=True),
        lax.psum_scatter(summed[15], "samp", scatter_dimension=0, tiled=True),
        lax.psum_scatter(summed[16], "samp", scatter_dimension=0, tiled=True),
        lax.psum_scatter(summed[17], "samp", scatter_dimension=0, tiled=True),
    )
    return (
        layer_output,
        input_grad,
        shares[0],
        shares[1],
        shares[2],
        shares[3],
        shares[4],
        shares[5],
        shares[6],
        shares[7],
        shares[8],
        shares[9],
        shares[10],
        shares[11],
        shares[12],
        shares[13],
        shares[14],
        shares[15],
        shares[16],
        shares[17],
    )


def solution(mesh):
    return jax.shard_map(
        local,
        mesh=mesh,
        in_specs=(
            P("samp", "feat", None),
            P(),
            P(),
            P(),
            P(),
            P(),
            P(),
            P(),
            P(),
            P(),
            P(),
            P(),
            P(),
            P(),
            P(),
            P(),
            P(),
            P(),
            P(),
            P(),
            P(),
            P("samp", "feat", None),
        ),
        out_specs=(
            P("samp", "feat", None),
            P("samp", "feat", None),
            P("samp"),
            P("samp"),
            P("samp", None),
            P("samp"),
            P("samp", None),
            P("samp"),
            P("samp"),
            P("samp"),
            P("samp", None),
            P("samp"),
            P("samp", None),
            P("samp"),
            P("samp"),
            P("samp"),
            P("samp", None),
            P("samp"),
            P("samp", None),
            P("samp"),
        ),
        check_vma=False,
    )
```

profile of v0, /device:TPU:0, one launch (start us, length us, event | category | flops | bytes accessed | tf_op | source)
XLA Modules:
  0.0 1231.0 jit_solution(3453029801898814704)
XLA Ops:
  33.9 98.7 %all-reduce.18.cloned.1.call-done = bf16[64,16,1024]{2,1,0:T(8,128)(2,1)} async-done(((bf16[64,16,1024]{2,1,0:T(8,128)(2,1)}), bf16[64,16,1024]{2,1,0:T(8,128)(2,1)}) %all-reduce.18.cloned.1.call-update) | async-done | bytes 2097168 | tf_op jit(solution)/shard_map/while/body/eval_jaxpr/psum | solution.py:15
  171.8 28.0 %all-gather.6.cloned.1.call-done = bf16[64,64,512]{2,1,0:T(8,128)(2,1)} async-done(((bf16[64,16,512]{2,1,0:T(8,128)(2,1)}), bf16[64,64,512]{2,1,0:T(8,128)(2,1)}) %all-gather.6.cloned.1.call-update) | async-done | bytes 4194320 | tf_op jit(solution)/shard_map/all_gather | solution.py:195
  199.8 11.4 reshape.299
  211.1 8.5 fusion.21
  224.9 11.6 all-gather.4.cloned.1.call-done
  236.5 11.2 reshape.297
  247.6 19.4 %convert_bitcast_fusion = bf16[64,16,8,64]{3,1,2,0:T(8,128)(2,1)} fusion(bf16[64,64,8,64]{3,2,1,0:T(8,128)(2,1)} %reshape.297, f32[64,8,16]{2,1,0:T(8,128)S(1)} %get-tuple-element.115, f32[64,8,16,64]{3,2,1,0:T(8,128)} %copy-done.10), kind=kOutput, calls=%fused_computation.111 | convolution fusion | flops 70262848 | bytes 7372800 | tf_op jit(solution)/shard_map/shfg,sghd->sfhd/dot_general | solution.py:76
  277.5 21.9 %multiply_convert_fusion = (bf16[64,16,2048]{2,1,0:T(8,128)(2,1)}, f32[64,16,2048]{2,1,0:T(8,128)S(1)}, f32[64,16,2048]{2,1,0:T(8,128)}) fusion(f32[2048]{0:T(1024)S(1)} %copy-done.73, bf16[512,2048]{1,0:T(8,128)(2,1)S(1)} %copy-done, f32[64,16,512]{2,1,0:T(8,128)S(1)} %get-tuple-element.118, f32[512]{0:T(512)S(1)} %copy-done.75, f32[512]{0:T(512)S(1)} %copy-done.65, ...), kind=kOutput, calls=%fused_computation.15 | convolution fusion | flops 2288517120 | bytes 25186304 | tf_op jit(solution)/shard_map/sfd,de->sfe/dot_general | solution.py:26
  299.4 7.9 convert_reduce_fusion
  318.5 23.3 %fusion.62 = f32[64,8,64,64]{3,2,1,0:T(8,128)} fusion(bf16[64,16,8,64]{3,2,1,0:T(8,128)(2,1)S(1)} %reshape.300, f32[64,8,16]{2,1,0:T(8,128)S(1)} %get-tuple-element.115, f32[64,8,16,64]{3,2,1,0:T(8,128)} %copy-done.10), kind=kOutput, calls=%fused_computation.126 | convolution fusion | flops 69738560 | bytes 11567104 | tf_op jit(solution)/shard_map/shfg,sfhd->sghd/dot_general | solution.py:108
  341.8 12.7 %copy.199 = f32[64,64,512]{2,1,0:T(8,128)} copy(f32[64,64,512]{1,2,0:T(8,128)} %bitcast.119) | data formatting | bytes 16777216 | tf_op jit(solution)/shard_map/reshape | solution.py:55
  354.6 9.1 multiply_reduce_fusion.1
  373.6 12.9 %copy.197 = f32[64,64,512]{2,1,0:T(8,128)} copy(f32[64,64,512]{1,2,0:T(8,128)} %bitcast.116) | data formatting | bytes 16777216 | tf_op jit(solution)/shard_map/reshape | solution.py:55
  397.4 29.0 %reduce-scatter.12.cloned.1.call-done = f32[64,16,512]{2,1,0:T(8,128)} async-done(((f32[64,64,512]{2,1,0:T(8,128)}), f32[64,16,512]{2,1,0:T(8,128)}) %reduce-scatter.12.cloned.1.call-update) | async-done | bytes 2097168 | tf_op jit(solution)/shard_map/reduce_scatter | solution.py:229
  429.8 71.0 %reduce-scatter.10.cloned.1.call-done = f32[64,16,512]{2,1,0:T(8,128)} async-done(((f32[64,64,512]{2,1,0:T(8,128)}), f32[64,16,512]{2,1,0:T(8,128)}) %reduce-scatter.10.cloned.1.call-update) | async-done | bytes 2097168 | tf_op jit(solution)/shard_map/reduce_scatter | solution.py:228
  551.7 88.0 %reduce-scatter.14.cloned.1.call-done = f32[8,16,1024]{2,1,0:T(8,128)} async-done(((f32[64,16,1024]{2,1,0:T(8,128)}), f32[8,16,1024]{2,1,0:T(8,128)}) %reduce-scatter.14.cloned.1.call-update) | async-done | bytes 524304 | tf_op jit(solution)/shard_map/reduce_scatter | solution.py:281
  678.2 13.6 %all-gather.8.cloned.1.call-done = bf16[64,16,1024]{2,1,0:T(8,128)(2,1)} async-done(((bf16[8,16,1024]{2,1,0:T(8,128)(2,1)}), bf16[64,16,1024]{2,1,0:T(8,128)(2,1)}) %all-gather.8.cloned.1.call-update) | async-done | bytes 2097168 | tf_op jit(solution)/shard_map/all_gather | solution.py:282
  713.0 44.5 %reduce-scatter.22.cloned.1.call-done = f32[64,512]{1,0:T(8,128)} async-done(((f32[512,512]{1,0:T(8,128)}), f32[64,512]{1,0:T(8,128)}) %reduce-scatter.22.cloned.1.call-update) | async-done | bytes 131088 | tf_op jit(solution)/shard_map/reduce_scatter | solution.py:328
  757.5 90.7 %reduce-scatter.26.cloned.1.call-done = f32[256,512]{1,0:T(8,128)} async-done(((f32[2048,512]{1,0:T(8,128)}), f32[256,512]{1,0:T(8,128)}) %reduce-scatter.26.cloned.1.call-update) | async-done | bytes 524304 | tf_op jit(solution)/shard_map/reduce_scatter | solution.py:334
  848.3 91.8 %reduce-scatter.24.cloned.1.call-done = f32[64,2048]{1,0:T(8,128)} async-done(((f32[512,2048]{1,0:T(8,128)}), f32[64,2048]{1,0:T(8,128)}) %reduce-scatter.24.cloned.1.call-update) | async-done | bytes 524304 | tf_op jit(solution)/shard_map/reduce_scatter | solution.py:332
  940.0 66.6 %reduce-scatter.18.cloned.1.call-done = f32[64,512]{1,0:T(8,128)} async-done(((f32[512,512]{1,0:T(8,128)}), f32[64,512]{1,0:T(8,128)}) %reduce-scatter.18.cloned.1.call-update) | async-done | bytes 131088 | tf_op jit(solution)/shard_map/reduce_scatter | solution.py:322
  1006.6 77.3 %reduce-scatter.20.cloned.1.call-done = f32[64,1536]{1,0:T(8,128)} async-done(((f32[512,1536]{1,0:T(8,128)}), f32[64,1536]{1,0:T(8,128)}) %reduce-scatter.20.cloned.1.call-update) | async-done | bytes 393232 | tf_op jit(solution)/shard_map/reduce_scatter | solution.py:326
  1083.9 77.4 %reduce-scatter.16.cloned.1.call-done = f32[64,1536]{1,0:T(8,128)} async-done(((f32[512,1536]{1,0:T(8,128)}), f32[64,1536]{1,0:T(8,128)}) %reduce-scatter.16.cloned.1.call-update) | async-done | bytes 393232 | tf_op jit(solution)/shard_map/reduce_scatter | solution.py:320
  1162.6 35.6 %all-reduce.12 = (f32[512]{0:T(512)S(1)}, f32[512]{0:T(512)S(1)}, f32[1024]{0:T(1024)S(1)}, f32[512]{0:T(512)S(1)}, f32[512]{0:T(512)S(1)}, /*index=5*/f32[512]{...) all-reduce(f32[512]{0:T(512)S(1)} %get-tuple-element.50, ...), channel_id=5, replica_groups=mesh['samp'=8,'feat'=4] {'samp'}, use_global_device_ids=true, to_apply=%region_26.27.clone | all-reduce | flops 8704 | bytes 69632
  (310 shorter events, 249.3 us)
Async XLA Ops:
  7.2 270.0 %copy-start = (bf16[512,2048]{1,0:T(8,128)(2,1)S(1)}, bf16[512,2048]{1,0:T(8,128)(2,1)}, u32[]{:S(2)}) copy-start(bf16[512,2048]{1,0:T(8,128)(2,1)} %param.39) | copy-start | bytes 6291460
  7.2 125.4 %all-reduce.18.cloned.1.call-start = ((), (), s32[]{:S(2)}) async-start(), calls=%async_computation.9 | async-start | bytes 4194304 | tf_op jit(solution)/shard_map/while/body/eval_jaxpr/psum | solution.py:15
  27.9 171.9 %all-gather.6.cloned.1.call-start = ((), (), s32[]{:S(2)}) async-start(), calls=%async_computation.11 | async-start | bytes 5242880 | tf_op jit(solution)/shard_map/all_gather | solution.py:195
  165.4 71.0 %all-gather.4.cloned.1.call-start = ((), (), s32[]{:S(2)}) async-start(), calls=%async_computation.10 | async-start | bytes 5242880 | tf_op jit(solution)/shard_map/all_gather | solution.py:196
  169.4 257.0 %reduce-scatter.12.cloned.1.call-start = ((), (), s32[]{:S(2)}) async-start(), calls=%async_computation.13 | async-start | bytes 10485760 | tf_op jit(solution)/shard_map/reduce_scatter | solution.py:229
  276.7 34.0 %copy-start.5 = (f32[64,16,512]{2,1,0:T(8,128)}, f32[64,16,512]{2,1,0:T(8,128)S(1)}, u32[]{:S(2)}) copy-start(f32[64,16,512]{2,1,0:T(8,128)S(1)} %get-tuple-element.118) | copy-start | bytes 6291460
  277.5 21.9 %copy-start.26 = (bf16[64,16,512]{2,1,0:T(8,128)(2,1)S(1)}, bf16[64,16,512]{2,1,0:T(8,128)(2,1)}, u32[]{:S(2)}) copy-start(bf16[64,16,512]{2,1,0:T(8,128)(2,1)} %param.43) | copy-start | bytes 3145732
  277.5 21.9 %copy-start.70 = (bf16[2048,512]{1,0:T(8,128)(2,1)S(1)}, bf16[2048,512]{1,0:T(8,128)(2,1)}, u32[]{:S(2)}) copy-start(bf16[2048,512]{1,0:T(8,128)(2,1)} %param.41) | copy-start | bytes 6291460
  354.5 146.2 %reduce-scatter.10.cloned.1.call-start = ((), (), s32[]{:S(2)}) async-start(), calls=%async_computation.12 | async-start | bytes 10485760 | tf_op jit(solution)/shard_map/reduce_scatter | solution.py:228
  354.5 9.1 copy-start.11
  386.5 253.2 %reduce-scatter.14.cloned.1.call-start = ((), (), s32[]{:S(2)}) async-start(), calls=%async_computation.14 | async-start | bytes 4718592 | tf_op jit(solution)/shard_map/reduce_scatter | solution.py:281
  426.4 76.2 %copy-start.36 = (f32[64,16]{1,0:T(8,128)S(1)}, f32[64,16]{1,0:T(8,128)}, u32[]{:S(2)}) copy-start(f32[64,16]{1,0:T(8,128)} %copy-done.35) | copy-start | bytes 12292
  426.4 76.2 %copy-start.59 = (f32[512]{0:T(512)S(1)}, f32[512]{0:T(512)}, u32[]{:S(2)}) copy-start(f32[512]{0:T(512)} %param.31) | copy-start | bytes 6148
  429.8 72.9 %copy-start.3 = (f32[64,16,512]{2,1,0:T(8,128)S(1)}, f32[64,16,512]{2,1,0:T(8,128)}, u32[]{:S(2)}) copy-start(f32[64,16,512]{2,1,0:T(8,128)} %copy-done.2) | copy-start | bytes 6291460
  551.7 90.0 %copy-start.23 = (bf16[64,16,512]{2,1,0:T(8,128)(2,1)S(1)}, bf16[64,16,512]{2,1,0:T(8,128)(2,1)}, u32[]{:S(2)}) copy-start(bf16[64,16,512]{2,1,0:T(8,128)(2,1)} %copy-done.22) | copy-start | bytes 3145732
  551.7 140.1 %all-gather.8.cloned.1.call-start = ((), (), s32[]{:S(2)}) async-start(), calls=%async_computation.15 | async-start | bytes 2359296 | tf_op jit(solution)/shard_map/all_gather | solution.py:282
  641.6 115.9 %reduce-scatter.22.cloned.1.call-start = ((), (), s32[]{:S(2)}) async-start(), calls=%async_computation.19 | async-start | bytes 1179648 | tf_op jit(solution)/shard_map/reduce_scatter | solution.py:328
  644.6 203.7 %reduce-scatter.26.cloned.1.call-start = ((), (), s32[]{:S(2)}) async-start(), calls=%async_computation.21 | async-start | bytes 4718592 | tf_op jit(solution)/shard_map/reduce_scatter | solution.py:334
  651.4 288.6 %reduce-scatter.24.cloned.1.call-start = ((), (), s32[]{:S(2)}) async-start(), calls=%async_computation.20 | async-start | bytes 4718592 | tf_op jit(solution)/shard_map/reduce_scatter | solution.py:332
  659.4 347.2 %reduce-scatter.18.cloned.1.call-start = ((), (), s32[]{:S(2)}) async-start(), calls=%async_computation.17 | async-start | bytes 1179648 | tf_op jit(solution)/shard_map/reduce_scatter | solution.py:322
  664.1 419.8 %reduce-scatter.20.cloned.1.call-start = ((), (), s32[]{:S(2)}) async-start(), calls=%async_computation.18 | async-start | bytes 3538944 | tf_op jit(solution)/shard_map/reduce_scatter | solution.py:326
  669.4 491.9 %reduce-scatter.16.cloned.1.call-start = ((), (), s32[]{:S(2)}) async-start(), calls=%async_computation.16 | async-start | bytes 3538944 | tf_op jit(solution)/shard_map/reduce_scatter | solution.py:320
  697.9 518.0 %all-reduce.20.cloned.1.call-start = ((), (), s32[]{:S(2)}) async-start(), calls=%async_computation.22 | async-start | bytes 4194304 | tf_op jit(solution)/shard_map/psum | solution.py:294
  1215.8 8.4 copy-start.1
  (74 other events, 219.0 us)
Sparse Core Ops, SparseCore 0:
  28.0 104.5 all-reduce.17
  165.5 34.1 all-gather.5
  201.9 34.4 all-gather.3
  354.6 71.7 reduce-scatter.11
  429.0 71.6 reduce-scatter.9
  551.8 87.9 reduce-scatter.13
  642.7 49.0 all-gather.7
  695.6 61.9 reduce-scatter.21
  761.1 87.0 reduce-scatter.25
  852.2 87.8 reduce-scatter.23
  943.5 63.0 reduce-scatter.17
  1010.5 73.4 reduce-scatter.19
  1087.9 73.3 reduce-scatter.15
  1164.1 51.6 all-reduce.19
where the time goes:
time: 1240 us; the launch traced here: 1230 us
  waiting for transfers between devices  795 us (64%)
  matrix products  188 us (15%)
  local copies, waits for them, and re-layouts  132 us (11%)
  other arithmetic  52.2 us (4%)
  blocking collectives  42.5 us (3%)
  between operations  19.7 us (2%)
    psum x1, waiting for transfers between devices, spread_2(): return lax.psum(block, axis)  98.7 us
    reduce_scatter x1, waiting for transfers between devices, local(): lax.psum_scatter(summed[14], 'samp', scatter_dimension=0, tiled=True)  91.8 us
    reduce_scatter x1, waiting for transfers between devices, local(): lax.psum_scatter(summed[16], 'samp', scatter_dimension=0, tiled=True)  90.7 us
    reduce_scatter x1, waiting for transfers between devices, local(): lax.psum_scatter(term_block, 'samp', scatter_dimension=0, tiled=True)  88 us
    reduce_scatter x1, waiting for transfers between devices, local(): lax.psum_scatter(summed[2], 'samp', scatter_dimension=0, tiled=True)  77.4 us
    reduce_scatter x1, waiting for transfers between devices, local(): lax.psum_scatter(summed[8], 'samp', scatter_dimension=0, tiled=True)  77.3 us
    reduce_scatter x1, waiting for transfers between devices, local(): lax.psum_scatter(grad_keys, 'feat', scatter_dimension=1, tiled=True)  71 us
    reduce_scatter x1, waiting for transfers between devices, local(): lax.psum_scatter(summed[4], 'samp', scatter_dimension=0, tiled=True)  66.6 us
  transfers between devices with their start and end apart: 14, of which 14 were waited for; matrix products, arithmetic and copies ran while one was open for 11% of the time, Pallas kernels for 0%

commit v1 on v0

--- a/solution.py
+++ b/solution.py
@@ -3,16 +3,18 @@
 import jax.numpy as jnp
 from jax import lax
 from jax.sharding import PartitionSpec as P
+from jax.lax import all_gather
 
 HEADS = 8
 HEAD_DIM = 64
 EPS = 1e-05
 MASKED = -1000000000.0
+answer_works = lambda unit, a_name: all_gather(unit, a_name).sum(axis=0)
 
 
 def spread_2(block, axis, owner):
     block = jnp.where(lax.axis_index(axis) == owner, block, jnp.zeros_like(block))
-    return lax.psum(block, axis)
+    return answer_works(block, axis)
 
 
 def layer_norm(values, gain_row, shift_row):

time: 1240 us -> 1370 us (1.10)
  waiting for transfers between devices: 795 us -> 920 us
    all_gather x0 -> x1, waiting for transfers between devices: none -> 224 us  [answer_works = lambda unit, a_name: all_gather(unit, a_name).sum(axis=0)]
    psum x1 -> x0, waiting for transfers between devices: 98.7 us -> none  [spread_2(): return lax.psum(block, axis)]
    reshape x8 -> x7, local copies, waits for them, and re-layouts: 40.7 us -> 37.1 us  [split_heads(): return values.reshape(values.shape[0], values.shape[1], HEADS, HEAD_DIM)]
  transfers between devices with their start and end apart: 14 -> 14, of which waited for: 14 -> 14; matrix products, arithmetic and copies ran while one was open for 11% -> 10% of each run, Pallas kernels for 0% -> 0%
where the time goes in v1:
time: 1370 us; the launch traced here: 1360 us
  waiting for transfers between devices  920 us (67%)
  matrix products  186 us (14%)
  local copies, waits for them, and re-layouts  131 us (10%)
  other arithmetic  63.1 us (5%)
  blocking collectives  42.5 us (3%)
  between operations  19.9 us (1%)
    all_gather x1, waiting for transfers between devices, answer_works = lambda unit, a_name: all_gather(unit, a_name).sum(axis=0)  224 us
    reduce_scatter x1, waiting for transfers between devices, local(): lax.psum_scatter(summed[14], 'samp', scatter_dimension=0, tiled=True)  91.6 us
    reduce_scatter x1, waiting for transfers between devices, local(): lax.psum_scatter(summed[16], 'samp', scatter_dimension=0, tiled=True)  90.8 us
    reduce_scatter x1, waiting for transfers between devices, local(): lax.psum_scatter(term_block, 'samp', scatter_dimension=0, tiled=True)  88.2 us
    reduce_scatter x1, waiting for transfers between devices, local(): lax.psum_scatter(summed[8], 'samp', scatter_dimension=0, tiled=True)  77.4 us
    reduce_scatter x1, waiting for transfers between devices, local(): lax.psum_scatter(summed[2], 'samp', scatter_dimension=0, tiled=True)  77.4 us
    reduce_scatter x1, waiting for transfers between devices, local(): lax.psum_scatter(grad_keys, 'feat', scatter_dimension=1, tiled=True)  71 us
    reduce_scatter x1, waiting for transfers between devices, local(): lax.psum_scatter(summed[4], 'samp', scatter_dimension=0, tiled=True)  66.6 us
  transfers between devices with their start and end apart: 14, of which 14 were waited for; matrix products, arithmetic and copies ran while one was open for 10% of the time, Pallas kernels for 0%

profile of v1, /device:TPU:0, one launch (start us, length us, event | category | flops | bytes accessed | tf_op | source)
XLA Modules:
  0.0 1364.1 jit_solution(15496879198896697891)
XLA Ops:
  33.9 224.5 %all-gather.5.cloned.1.call-done = bf16[8,64,16,1024]{3,2,1,0:T(8,128)(2,1)} async-done(((bf16[1,64,16,1024]{3,2,1,0:T(8,128)(2,1)}), bf16[8,64,16,1024]{3,2,1,0:T(8,128)(2,1)}) %all-gather.5.cloned.1.call-update) | async-done | bytes 16777232 | tf_op jit(solution)/shard_map/while/body/eval_jaxpr/all_gather | solution.py:12
  258.4 10.8 reduce_sum.303
  307.2 26.5 %all-gather.9.cloned.1.call-done = bf16[64,64,512]{2,1,0:T(8,128)(2,1)} async-done(((bf16[64,16,512]{2,1,0:T(8,128)(2,1)}), bf16[64,64,512]{2,1,0:T(8,128)(2,1)}) %all-gather.9.cloned.1.call-update) | async-done | bytes 4194320 | tf_op jit(solution)/shard_map/all_gather | solution.py:197
  333.7 11.4 reshape.328
  345.1 8.5 fusion.21
  358.8 11.6 all-gather.7.cloned.1.call-done
  370.4 11.2 reshape.326
  381.5 19.2 %convert_bitcast_fusion = bf16[64,16,8,64]{3,1,2,0:T(8,128)(2,1)} fusion(bf16[64,64,8,64]{3,2,1,0:T(8,128)(2,1)} %reshape.326, f32[64,8,16]{2,1,0:T(8,128)S(1)} %get-tuple-element.115, f32[64,8,16,64]{3,2,1,0:T(8,128)} %copy-done.10), kind=kOutput, calls=%fused_computation.111 | convolution fusion | flops 70262848 | bytes 7372800 | tf_op jit(solution)/shard_map/shfg,sghd->sfhd/dot_general | solution.py:78
  411.2 21.9 %multiply_convert_fusion = (bf16[64,16,2048]{2,1,0:T(8,128)(2,1)}, f32[64,16,2048]{2,1,0:T(8,128)S(1)}, f32[64,16,2048]{2,1,0:T(8,128)}) fusion(f32[2048]{0:T(1024)S(1)} %copy-done.73, bf16[512,2048]{1,0:T(8,128)(2,1)S(1)} %copy-done, f32[64,16,512]{2,1,0:T(8,128)S(1)} %get-tuple-element.118, f32[512]{0:T(512)S(1)} %copy-done.75, f32[512]{0:T(512)S(1)} %copy-done.65, ...), kind=kOutput, calls=%fused_computation.15 | convolution fusion | flops 2288517120 | bytes 25186304 | tf_op jit(solution)/shard_map/sfd,de->sfe/dot_general | solution.py:28
  452.4 23.3 %fusion.59 = f32[64,8,64,64]{3,2,1,0:T(8,128)} fusion(bf16[64,16,8,64]{3,2,1,0:T(8,128)(2,1)S(1)} %reshape.329, f32[64,8,16]{2,1,0:T(8,128)S(1)} %get-tuple-element.115, f32[64,8,16,64]{3,2,1,0:T(8,128)} %copy-done.10), kind=kOutput, calls=%fused_computation.123 | convolution fusion | flops 69738560 | bytes 11567104 | tf_op jit(solution)/shard_map/shfg,sfhd->sghd/dot_general | solution.py:110
  475.7 12.7 copy.164
  488.5 9.1 multiply_reduce_fusion.1
  507.6 12.9 copy.162
  531.3 29.0 %reduce-scatter.12.cloned.1.call-done = f32[64,16,512]{2,1,0:T(8,128)} async-done(((f32[64,64,512]{2,1,0:T(8,128)}), f32[64,16,512]{2,1,0:T(8,128)}) %reduce-scatter.12.cloned.1.call-update) | async-done | bytes 2097168 | tf_op jit(solution)/shard_map/reduce_scatter | solution.py:231
  563.7 71.0 %reduce-scatter.10.cloned.1.call-done = f32[64,16,512]{2,1,0:T(8,128)} async-done(((f32[64,64,512]{2,1,0:T(8,128)}), f32[64,16,512]{2,1,0:T(8,128)}) %reduce-scatter.10.cloned.1.call-update) | async-done | bytes 2097168 | tf_op jit(solution)/shard_map/reduce_scatter | solution.py:230
  684.4 88.2 %reduce-scatter.14.cloned.1.call-done = f32[8,16,1024]{2,1,0:T(8,128)} async-done(((f32[64,16,1024]{2,1,0:T(8,128)}), f32[8,16,1024]{2,1,0:T(8,128)}) %reduce-scatter.14.cloned.1.call-update) | async-done | bytes 524304 | tf_op jit(solution)/shard_map/reduce_scatter | solution.py:283
  810.8 13.7 %all-gather.11.cloned.1.call-done = bf16[64,16,1024]{2,1,0:T(8,128)(2,1)} async-done(((bf16[8,16,1024]{2,1,0:T(8,128)(2,1)}), bf16[64,16,1024]{2,1,0:T(8,128)(2,1)}) %all-gather.11.cloned.1.call-update) | async-done | bytes 2097168 | tf_op jit(solution)/shard_map/all_gather | solution.py:284
  845.8 44.5 %reduce-scatter.22.cloned.1.call-done = f32[64,512]{1,0:T(8,128)} async-done(((f32[512,512]{1,0:T(8,128)}), f32[64,512]{1,0:T(8,128)}) %reduce-scatter.22.cloned.1.call-update) | async-done | bytes 131088 | tf_op jit(solution)/shard_map/reduce_scatter | solution.py:330
  890.3 90.8 %reduce-scatter.26.cloned.1.call-done = f32[256,512]{1,0:T(8,128)} async-done(((f32[2048,512]{1,0:T(8,128)}), f32[256,512]{1,0:T(8,128)}) %reduce-scatter.26.cloned.1.call-update) | async-done | bytes 524304 | tf_op jit(solution)/shard_map/reduce_scatter | solution.py:336
  981.1 91.6 %reduce-scatter.24.cloned.1.call-done = f32[64,2048]{1,0:T(8,128)} async-done(((f32[512,2048]{1,0:T(8,128)}), f32[64,2048]{1,0:T(8,128)}) %reduce-scatter.24.cloned.1.call-update) | async-done | bytes 524304 | tf_op jit(solution)/shard_map/reduce_scatter | solution.py:334
  1072.7 66.6 %reduce-scatter.18.cloned.1.call-done = f32[64,512]{1,0:T(8,128)} async-done(((f32[512,512]{1,0:T(8,128)}), f32[64,512]{1,0:T(8,128)}) %reduce-scatter.18.cloned.1.call-update) | async-done | bytes 131088 | tf_op jit(solution)/shard_map/reduce_scatter | solution.py:324
  1139.3 77.4 %reduce-scatter.20.cloned.1.call-done = f32[64,1536]{1,0:T(8,128)} async-done(((f32[512,1536]{1,0:T(8,128)}), f32[64,1536]{1,0:T(8,128)}) %reduce-scatter.20.cloned.1.call-update) | async-done | bytes 393232 | tf_op jit(solution)/shard_map/reduce_scatter | solution.py:328
  1216.8 77.4 %reduce-scatter.16.cloned.1.call-done = f32[64,1536]{1,0:T(8,128)} async-done(((f32[512,1536]{1,0:T(8,128)}), f32[64,1536]{1,0:T(8,128)}) %reduce-scatter.16.cloned.1.call-update) | async-done | bytes 393232 | tf_op jit(solution)/shard_map/reduce_scatter | solution.py:322
  1295.5 35.6 %all-reduce.12 = (f32[512]{0:T(512)S(1)}, f32[512]{0:T(512)S(1)}, f32[1024]{0:T(1024)S(1)}, f32[512]{0:T(512)S(1)}, f32[512]{0:T(512)S(1)}, /*index=5*/f32[512]{...) all-reduce(f32[512]{0:T(512)S(1)} %get-tuple-element.50, ...), channel_id=5, replica_groups=mesh['samp'=8,'feat'=4] {'samp'}, use_global_device_ids=true, to_apply=%region_26.27.clone | all-reduce | flops 8704 | bytes 69632
  (311 shorter events, 254.8 us)
Async XLA Ops:
  7.2 403.7 %copy-start = (bf16[512,2048]{1,0:T(8,128)(2,1)S(1)}, bf16[512,2048]{1,0:T(8,128)(2,1)}, u32[]{:S(2)}) copy-start(bf16[512,2048]{1,0:T(8,128)(2,1)} %param.39) | copy-start | bytes 6291460
  7.2 251.2 %all-gather.5.cloned.1.call-start = ((), (), s32[]{:S(2)}) async-start(), calls=%async_computation.9 | async-start | bytes 18874368 | tf_op jit(solution)/shard_map/while/body/eval_jaxpr/all_gather | solution.py:12
  27.9 305.8 %all-gather.9.cloned.1.call-start = ((), (), s32[]{:S(2)}) async-start(), calls=%async_computation.11 | async-start | bytes 5242880 | tf_op jit(solution)/shard_map/all_gather | solution.py:197
  300.9 69.5 %all-gather.7.cloned.1.call-start = ((), (), s32[]{:S(2)}) async-start(), calls=%async_computation.10 | async-start | bytes 5242880 | tf_op jit(solution)/shard_map/all_gather | solution.py:198
  304.8 255.5 %reduce-scatter.12.cloned.1.call-start = ((), (), s32[]{:S(2)}) async-start(), calls=%async_computation.13 | async-start | bytes 10485760 | tf_op jit(solution)/shard_map/reduce_scatter | solution.py:231
  410.4 34.0 %copy-start.5 = (f32[64,16,512]{2,1,0:T(8,128)}, f32[64,16,512]{2,1,0:T(8,128)S(1)}, u32[]{:S(2)}) copy-start(f32[64,16,512]{2,1,0:T(8,128)S(1)} %get-tuple-element.118) | copy-start | bytes 6291460
  411.2 21.9 %copy-start.26 = (bf16[64,16,512]{2,1,0:T(8,128)(2,1)S(1)}, bf16[64,16,512]{2,1,0:T(8,128)(2,1)}, u32[]{:S(2)}) copy-start(bf16[64,16,512]{2,1,0:T(8,128)(2,1)} %param.43) | copy-start | bytes 3145732
  411.2 21.9 %copy-start.70 = (bf16[2048,512]{1,0:T(8,128)(2,1)S(1)}, bf16[2048,512]{1,0:T(8,128)(2,1)}, u32[]{:S(2)}) copy-start(bf16[2048,512]{1,0:T(8,128)(2,1)} %param.41) | copy-start | bytes 6291460
  488.4 146.2 %reduce-scatter.10.cloned.1.call-start = ((), (), s32[]{:S(2)}) async-start(), calls=%async_computation.12 | async-start | bytes 10485760 | tf_op jit(solution)/shard_map/reduce_scatter | solution.py:230
  488.5 9.1 copy-start.11
  520.5 252.0 %reduce-scatter.14.cloned.1.call-start = ((), (), s32[]{:S(2)}) async-start(), calls=%async_computation.14 | async-start | bytes 4718592 | tf_op jit(solution)/shard_map/reduce_scatter | solution.py:283
  560.3 76.2 %copy-start.36 = (f32[64,16]{1,0:T(8,128)S(1)}, f32[64,16]{1,0:T(8,128)}, u32[]{:S(2)}) copy-start(f32[64,16]{1,0:T(8,128)} %copy-done.35) | copy-start | bytes 12292
  560.3 76.2 %copy-start.59 = (f32[512]{0:T(512)S(1)}, f32[512]{0:T(512)}, u32[]{:S(2)}) copy-start(f32[512]{0:T(512)} %param.31) | copy-start | bytes 6148
  563.7 72.9 %copy-start.3 = (f32[64,16,512]{2,1,0:T(8,128)S(1)}, f32[64,16,512]{2,1,0:T(8,128)}, u32[]{:S(2)}) copy-start(f32[64,16,512]{2,1,0:T(8,128)} %copy-done.2) | copy-start | bytes 6291460
  684.3 90.1 %copy-start.23 = (bf16[64,16,512]{2,1,0:T(8,128)(2,1)S(1)}, bf16[64,16,512]{2,1,0:T(8,128)(2,1)}, u32[]{:S(2)}) copy-start(bf16[64,16,512]{2,1,0:T(8,128)(2,1)} %copy-done.22) | copy-start | bytes 3145732
  684.3 140.2 %all-gather.11.cloned.1.call-start = ((), (), s32[]{:S(2)}) async-start(), calls=%async_computation.15 | async-start | bytes 2359296 | tf_op jit(solution)/shard_map/all_gather | solution.py:284
  774.3 116.0 %reduce-scatter.22.cloned.1.call-start = ((), (), s32[]{:S(2)}) async-start(), calls=%async_computation.19 | async-start | bytes 1179648 | tf_op jit(solution)/shard_map/reduce_scatter | solution.py:330
  777.3 203.8 %reduce-scatter.26.cloned.1.call-start = ((), (), s32[]{:S(2)}) async-start(), calls=%async_computation.21 | async-start | bytes 4718592 | tf_op jit(solution)/shard_map/reduce_scatter | solution.py:336
  784.2 288.5 %reduce-scatter.24.cloned.1.call-start = ((), (), s32[]{:S(2)}) async-start(), calls=%async_computation.20 | async-start | bytes 4718592 | tf_op jit(solution)/shard_map/reduce_scatter | solution.py:334
  792.2 347.1 %reduce-scatter.18.cloned.1.call-start = ((), (), s32[]{:S(2)}) async-start(), calls=%async_computation.17 | async-start | bytes 1179648 | tf_op jit(solution)/shard_map/reduce_scatter | solution.py:324
  796.7 420.1 %reduce-scatter.20.cloned.1.call-start = ((), (), s32[]{:S(2)}) async-start(), calls=%async_computation.18 | async-start | bytes 3538944 | tf_op jit(solution)/shard_map/reduce_scatter | solution.py:328
  802.0 492.2 %reduce-scatter.16.cloned.1.call-start = ((), (), s32[]{:S(2)}) async-start(), calls=%async_computation.16 | async-start | bytes 3538944 | tf_op jit(solution)/shard_map/reduce_scatter | solution.py:322
  830.6 518.1 %all-reduce.17.cloned.1.call-start = ((), (), s32[]{:S(2)}) async-start(), calls=%async_computation.22 | async-start | bytes 4194304 | tf_op jit(solution)/shard_map/psum | solution.py:296
  1348.7 8.4 copy-start.1
  (74 other events, 215.6 us)
Sparse Core Ops, SparseCore 0:
  28.1 230.3 all-gather.4
  301.0 32.6 all-gather.8
  335.9 34.4 all-gather.6
  488.6 71.7 reduce-scatter.11
  562.9 71.6 reduce-scatter.9
  684.4 88.0 reduce-scatter.13
  775.4 49.0 all-gather.10
  828.3 61.9 reduce-scatter.21
  894.0 87.0 reduce-scatter.25
  985.0 87.6 reduce-scatter.23
  1076.1 63.1 reduce-scatter.17
  1143.2 73.5 reduce-scatter.19
  1220.8 73.3 reduce-scatter.15
  1297.0 51.6 all-reduce.16
